TPU v7x, 32 devices: a whole 2x2x4 slice. The times are simulated.
32 devices in a mesh: dp: 4 (over y, core), seq: 8 (over z, x).
Axes of the slice: x: 2, y: 2, z: 4, core: 2. Of those that a mesh axis runs over, the one named last changes fastest.
Arguments:
- layer_input: bfloat16 [4096, 8192], P(('dp', 'seq')), may hold values from -6 to 6
- queries: bfloat16 [4096, 4096], P(('dp', 'seq')), may hold values from -110 to 110, as said below
- key_states: bfloat16 [4096, 512], P(('dp', 'seq')), may hold values from -12 to 12, as said below
- value_states: bfloat16 [4096, 512], P(('dp', 'seq')), may hold values from -6 to 6
- out_grad: bfloat16 [4096, 4096], P(('dp', 'seq')), may hold values from -6 to 6
Outputs:
- query_grad: bfloat16 [4096, 4096], P(('dp', 'seq'))
- key_grad: bfloat16 [4096, 512], P(('dp', 'seq'))
- value_grad: bfloat16 [4096, 512], P(('dp', 'seq'))
- weight_grad: float32 [8192, 1024], P(('dp', 'seq'))
Inputs may be any that keep to these rules, and one draw needn't show every extreme that they name: `queries`: rows of rough scales; some queries may nearly coincide in direction with keys of earlier positions. `key_states`: rows of rough scales.
All inputs are finite; a program needn't handle non-finite values.
Results may differ from a plain program's by a relative error of at most 0.0051.
Values may be sent and summed in bfloat16 or wider, within the bound.
No kernel may reach another device: no remote copies, remote signals or barrier semaphores. Data moves between devices by JAX's collectives and lax.ppermute only.
A program may use at most 128 MiB of HBM per device.

v0:
```python
import math
import jax
import jax.numpy as jnp
from jax import lax
from jax.sharding import PartitionSpec as P

D = 8192
QH = 32
KVH = 4
HD = 128
NEGATIVE = -1e30


def local(layer_input, queries, key_states, value_states, out_grad):
    local_rows = layer_input.shape[0]
    cycle_size = lax.axis_size("seq")
    replicas = lax.axis_size("dp")
    position = lax.axis_index("seq")
    length = local_rows * cycle_size
    group = QH // KVH
    channels = KVH * HD
    scale = 1.0 / math.sqrt(HD)
    block = math.gcd(length, 512)
    key_all, value_all = (
        lax.all_gather(key_states, "seq", axis=0, tiled=True),
        lax.all_gather(value_states, "seq", axis=0, tiled=True),
    )
    query_heads = queries.reshape(local_rows, KVH, group, HD)
    grad_heads = out_grad.reshape(local_rows, KVH, group, HD)
    query_place = position * local_rows + jnp.arange(local_rows, dtype=jnp.int32)
    needed = (position * local_rows + local_rows + block - 1) // block

    def block_scores(begin):
        key_block = lax.dynamic_slice_in_dim(key_all, begin, block, 0).reshape(block, KVH, HD)
        value_block = lax.dynamic_slice_in_dim(value_all, begin, block, 0).reshape(block, KVH, HD)
        scores = (
            jnp.einsum("tkgd,skd->kgts", query_heads, key_block, preferred_element_type=jnp.float32)
            * scale
        )
        key_place = begin + jnp.arange(block, dtype=jnp.int32)
        visible = key_place[None, :] <= query_place[:, None]
        scores = jnp.where(visible, scores, NEGATIVE)
        grad_probs = jnp.einsum(
            "tkgd,skd->kgts", grad_heads, value_block, preferred_element_type=jnp.float32
        )
        return (key_block, scores, grad_probs)

    def first_pass(step_index, carry):
        row_max, denom, weighted = carry
        key_block, scores, grad_probs = block_scores(step_index * block)
        new_max = jnp.maximum(row_max, jnp.max(scores, axis=-1))
        factor = jnp.exp(row_max - new_max)
        expon = jnp.exp(scores - new_max[..., None])
        return (
            new_max,
            denom * factor + jnp.sum(expon, axis=-1),
            weighted * factor + jnp.sum(expon * grad_probs, axis=-1),
        )

    stats_shape = (KVH, group, local_rows)
    start_stats = (
        jnp.full(stats_shape, NEGATIVE, jnp.float32),
        jnp.zeros(stats_shape, jnp.float32),
        jnp.zeros(stats_shape, jnp.float32),
    )
    row_max, denom, weighted = lax.fori_loop(0, needed, first_pass, start_stats)
    delta = weighted / denom

    def second_pass(step_index, carry):
        grad_query, terms = carry
        begin = step_index * block
        key_block, scores, grad_probs = block_scores(begin)
        probs = jnp.exp(scores - row_max[..., None]) / denom[..., None]
        grad_scores = (scale * probs * (grad_probs - delta[..., None])).astype(jnp.bfloat16)
        probs_low = probs.astype(jnp.bfloat16)
        grad_query = grad_query + jnp.einsum(
            "kgts,skd->tkgd", grad_scores, key_block, preferred_element_type=jnp.float32
        )
        key_part = jnp.einsum(
            "kgts,tkgd->skd", grad_scores, query_heads, preferred_element_type=jnp.float32
        )
        value_part = jnp.einsum(
            "kgts,tkgd->skd", probs_low, grad_heads, preferred_element_type=jnp.float32
        )
        joined = jnp.concatenate(
            [key_part.reshape(block, channels), value_part.reshape(block, channels)], axis=1
        )
        terms = lax.dynamic_update_slice_in_dim(terms, joined, begin, 0)
        return (grad_query, terms)

    start_grads = (
        jnp.zeros((local_rows, KVH, group, HD), jnp.float32),
        jnp.zeros((length, 2 * channels), jnp.float32),
    )
    grad_query, terms = lax.fori_loop(0, needed, second_pass, start_grads)
    query_grad = grad_query.reshape(local_rows, QH * HD).astype(jnp.bfloat16)
    owned_grads = lax.psum_scatter(terms, "seq", scatter_dimension=0, tiled=True).astype(
        jnp.bfloat16
    )
    summed_grads = lax.all_gather(owned_grads, "seq", axis=0, tiled=True)
    slab = D // (replicas * cycle_size)
    columns = lax.all_to_all(
        layer_input.reshape(local_rows, replicas, cycle_size, slab),
        "seq",
        split_axis=2,
        concat_axis=0,
        tiled=True,
    )
    columns = columns.reshape(length, replicas * slab)
    weight_grad = lax.psum_scatter(
        jnp.einsum("tr,tc->rc", columns, summed_grads, preferred_element_type=jnp.float32),
        "dp",
        scatter_dimension=0,
        tiled=True,
    )
    return (query_grad, owned_grads[:, :channels], owned_grads[:, channels:], weight_grad)


def solution(mesh):
    in_specs = (
        P(("dp", "seq"), None),
        P(("dp", "seq"), None),
        P(("dp", "seq"), None),
        P(("dp", "seq"), None),
        P(("dp", "seq"), None),
    )
    out_specs = (
        P(("dp", "seq"), None),
        P(("dp", "seq"), None),
        P(("dp", "seq"), None),
        P(("dp", "seq"), None),
    )
    return jax.shard_map(local, mesh=mesh, in_specs=in_specs, out_specs=out_specs, check_vma=False)
```

profile of v0, /device:TPU:0, one launch (start us, length us, event | category | flops | bytes accessed | tf_op | source)
XLA Modules:
  0.0 388.9 jit_solution(6068416372018879133)
XLA Ops:
  7.2 0.0 all-gather.4.cloned.1.call-start
  7.2 1.7 copy.69
  8.9 0.0 all-gather.6.cloned.1.call-start
  8.9 1.7 copy.71
  10.6 0.0 reduce-scatter.3.cloned.1.call-start
  10.7 1.6 copy.70
  12.3 0.7 copy.73
  13.0 1.6 copy.72
  14.6 1.3 copy.74
  15.9 37.0 %all-gather.4.cloned.1.call-done = bf16[1024,512]{0,1:T(8,128)(2,1)} async-done(((bf16[128,512]{0,1:T(8,128)(2,1)}), bf16[1024,512]{0,1:T(8,128)(2,1)}) %all-gather.4.cloned.1.call-update) | async-done | bytes 1048592 | tf_op jit(solution)/shard_map/all_gather | solution.py:25
  52.9 41.1 %all-gather.6.cloned.1.call-done = bf16[1024,512]{0,1:T(8,128)(2,1)} async-done(((bf16[128,512]{0,1:T(8,128)(2,1)}), bf16[1024,512]{0,1:T(8,128)(2,1)}) %all-gather.6.cloned.1.call-update) | async-done | bytes 1048592 | tf_op jit(solution)/shard_map/all_gather | solution.py:26
  94.0 7.5 %while.28 = (s32[]{:T(128)}, f32[4,8,128]{2,1,0:T(8,128)S(1)}, f32[4,8,128]{2,1,0:T(8,128)S(1)}, f32[4,8,128]{2,1,0:T(8,128)S(1)}, s32[]{:T(128)}, /*index=5*/bf...) while((s32[]{:T(128)}, f32[4,8,128]{2,1,0:T(8,128)S(1)}, ...), condition=%wide.region_4.5_spmd.clone, body=%wide.region_0.4_spmd.clone.sunk | while | flops 1098986112 | bytes 35165400 | solution.py:66
  94.0 1.3 constant_dynamic-slice_fusion.6
  95.3 0.1 broadcast_compare_fusion.4
  95.4 1.5 fusion.57
  96.9 1.8 fusion.59
  98.7 2.7 fusion.58
  101.5 2.5 broadcast_in_dim.32.clone
  104.0 1.6 broadcast_in_dim.31
  105.6 19.8 %while.29 = (s32[]{:T(128)}, f32[128,4,8,128]{0,3,2,1:T(8,128)}, f32[1024,1024]{1,0:T(8,128)}, s32[]{:T(128)}, bf16[1024,512]{0,1:T(8,128)(2,1)}, /*index=5*/bf1...) while((s32[]{:T(128)}, f32[128,4,8,128]{0,3,2,1:T(8,128)}, ...), condition=%wide.region_6.7_spmd.clone, body=%wide.region_5.6_spmd.clone.sunk | while | flops 2704343552 | bytes 108713312 | solution.py:95
  105.6 1.6 constant_dynamic-slice_fusion.7
  107.3 0.1 broadcast_compare_fusion.5
  107.4 2.3 fusion.70
  109.8 1.7 fusion.71
  111.5 1.5 fusion.73
  113.0 0.5 copy-done
  113.4 1.5 fusion.72
  114.9 1.5 pad_maximum_fusion.2
  116.4 1.9 copy.110
  118.4 1.5 constant_dynamic-update-slice_fusion.2
  119.8 1.5 copy-done.1
  121.3 4.1 %bitcast_add_fusion.2 = f32[128,4,8,128]{0,3,2,1:T(8,128)} fusion(f32[128,4,8,128]{0,3,2,1:T(8,128)} %get-tuple-element.501, bf16[512,4,128,1]{0,2,3,1:T(8,128)(2,1)} %bitcast.153, bf16[4,8,128,512]{2,3,1,0:T(8,128)(2,1)S(1)} %copy-done.1), kind=kOutput, calls=%fused_computation.26.clone.1 | convolution fusion | flops 537395200 | bytes 8912896 | tf_op jit(solution)/shard_map/while/body/kgts,skd->tkgd/dot_general | solution.py:76
  125.4 3.2 copy.77
  128.6 1.5 copy.78
  130.1 30.8 %all-to-all-start = ((bf16[128,4,8,256]{0,3,1,2:T(8,128)(2,1)}), bf16[128,4,8,256]{0,3,1,2:T(8,128)(2,1)S(1)}, u32[]{:S(2)}, u32[]{:S(2)}) async-start(bf16[128,4,8,256]{0,3,1,2:T(8,128)(2,1)} %copy.78), calls=%async_computation.1 | async-start | bytes 4194304 | tf_op jit(solution)/shard_map/all_to_all | solution.py:102
  160.9 0.0 all-gather.8.cloned.1.call-start
  161.0 117.2 %reduce-scatter.3.cloned.1.call-done = f32[128,1024]{1,0:T(8,128)} async-done(((f32[1024,1024]{1,0:T(8,128)}), f32[128,1024]{1,0:T(8,128)}) %reduce-scatter.3.cloned.1.call-update) | async-done | bytes 524304 | tf_op jit(solution)/shard_map/reduce_scatter | solution.py:97
  278.2 1.8 convert_element_type.17
  280.0 0.3 reduce-scatter.5.cloned.1.call-start
  280.3 2.7 copy.79
  283.0 47.1 %all-gather.8.cloned.1.call-done = bf16[1024,1024]{1,0:T(8,128)(2,1)} async-done(((bf16[128,1024]{1,0:T(8,128)(2,1)}), bf16[1024,1024]{1,0:T(8,128)(2,1)}) %all-gather.8.cloned.1.call-update) | async-done | bytes 2097168 | tf_op jit(solution)/shard_map/all_gather | solution.py:100
  330.0 6.6 %convolution_bitcast_fusion = f32[1024,1024]{0,1:T(8,128)} fusion(bf16[1024,1024]{1,0:T(8,128)(2,1)} %all-gather.8.cloned.1.call-done, bf16[128,8,8,128]{3,2,1,0:T(8,128)(2,1)} %bitcast.159), kind=kOutput, calls=%fused_computation.33 | convolution fusion | flops 2147483648 | bytes 8388608 | tf_op jit(solution)/shard_map/tr,tc->rc/dot_general | solution.py:111
  336.6 1.6 copy-done.2
  338.2 0.2 convert_element_type.15
  338.4 1.3 copy.93
  339.7 0.7 fusion.16
  340.4 39.4 %reduce-scatter.5.cloned.1.call-done = f32[256,1024]{0,1:T(8,128)} async-done(((f32[1024,1024]{0,1:T(8,128)}), f32[256,1024]{0,1:T(8,128)}) %reduce-scatter.5.cloned.1.call-update) | async-done | bytes 1048592 | tf_op jit(solution)/shard_map/reduce_scatter | solution.py:110
  379.8 2.5 copy.80
  (30 shorter events, 0.2 us)
Async XLA Ops:
  7.2 45.7 %all-gather.4.cloned.1.call-start = ((), (), s32[]{:S(2)}) async-start(), calls=%async_computation.3 | async-start | bytes 1179648 | tf_op jit(solution)/shard_map/all_gather | solution.py:25
  8.9 85.1 %all-gather.6.cloned.1.call-start = ((), (), s32[]{:S(2)}) async-start(), calls=%async_computation.4 | async-start | bytes 1179648 | tf_op jit(solution)/shard_map/all_gather | solution.py:26
  10.6 267.5 %reduce-scatter.3.cloned.1.call-start = ((), (), s32[]{:S(2)}) async-start(), calls=%async_computation.5 | async-start | bytes 4718592 | tf_op jit(solution)/shard_map/reduce_scatter | solution.py:97
  96.9 1.8 copy-start.7
  105.6 5.8 %copy-start.3 = (bf16[128,4,8,128]{0,3,2,1:T(8,128)(2,1)}, bf16[128,4,8,128]{0,3,2,1:T(8,128)(2,1)S(1)}, u32[]{:S(2)}) copy-start(bf16[128,4,8,128]{0,3,2,1:T(8,128)(2,1)S(1)} %get-tuple-element.521) | copy-start | bytes 3145732 | tf_op jit(solution)/shard_map/while
  107.2 2.5 copy-start.5
  111.5 2.0 copy-start
  118.3 2.9 copy-start.1
  121.3 4.1 %copy-start.4 = (bf16[128,4,8,128]{0,3,2,1:T(8,128)(2,1)S(1)}, bf16[128,4,8,128]{0,3,2,1:T(8,128)(2,1)}, u32[]{:S(2)}) copy-start(bf16[128,4,8,128]{0,3,2,1:T(8,128)(2,1)} %copy-done.3) | copy-start | bytes 3145732 | tf_op jit(solution)/shard_map/while
  130.1 150.1 %all-to-all-start = ((bf16[128,4,8,256]{0,3,1,2:T(8,128)(2,1)}), bf16[128,4,8,256]{0,3,1,2:T(8,128)(2,1)S(1)}, u32[]{:S(2)}, u32[]{:S(2)}) async-start(bf16[128,4,8,256]{0,3,1,2:T(8,128)(2,1)} %copy.78), calls=%async_computation.1 | async-start | bytes 4194304 | tf_op jit(solution)/shard_map/all_to_all | solution.py:102
  160.9 169.1 %all-gather.8.cloned.1.call-start = ((), (), s32[]{:S(2)}) async-start(), calls=%async_computation.6 | async-start | bytes 2359296 | tf_op jit(solution)/shard_map/all_gather | solution.py:100
  280.0 99.8 %reduce-scatter.5.cloned.1.call-start = ((), (), s32[]{:S(2)}) async-start(), calls=%async_computation.7 | async-start | bytes 5242880 | tf_op jit(solution)/shard_map/reduce_scatter | solution.py:110
  336.6 1.6 copy-start.2
  336.6 3.1 copy-start.6
Sparse Core Ops, SparseCore 0:
  10.6 42.2 all-gather.3
  55.5 38.4 all-gather.5
  125.5 152.5 reduce-scatter.2
  280.9 49.0 all-gather.7
  336.8 42.9 reduce-scatter.4
where the time goes:
time: 390 us; the launch traced here: 389 us
  waiting for transfers between devices  282 us (72%)
  local copies, waits for them, and re-layouts  34.5 us (9%)
  starting transfers between devices  31.2 us (8%)
  matrix products  21.8 us (6%)
  between operations  13.9 us (4%)
  other arithmetic  5.56 us (1%)
    reduce_scatter x1, waiting for transfers between devices, local(): lax.psum_scatter(terms, 'seq', scatter_dimension=0, tiled=True)  117 us
    all_gather x1, waiting for transfers between devices, local(): summed_grads = lax.all_gather(owned_grads, 'seq', axis=0, tiled=True)  47.1 us
    all_gather x1, waiting for transfers between devices, local(): lax.all_gather(value_states, 'seq', axis=0, tiled=True)  41.1 us
    reduce_scatter x1, waiting for transfers between devices, local(): lax.psum_scatter(jnp.einsum('tr,tc->rc', columns, summed_grads, preferred...  39.4 us
    all_gather x1, waiting for transfers between devices, local(): lax.all_gather(key_states, 'seq', axis=0, tiled=True)  37 us
    all_to_all x1, starting transfers between devices, local(): lax.all_to_all(layer_input.reshape(local_rows, replicas, cycle_size, slab...  30.8 us
    unnamed x12, local copies, waits for them, and re-layouts  15.9 us
  transfers between devices with their start and end apart: 6, of which 5 were waited for; matrix products, arithmetic and copies ran while one was open for 5% of the time, Pallas kernels for 0%

commit v1 on v0

--- a/solution.py
+++ b/solution.py
@@ -11,6 +11,28 @@
 NEGATIVE = -1e30
 
 
+def in_order(blocks, dim):
+    lengths = list(blocks.shape[1:])
+    lengths[dim] *= blocks.shape[0]
+    return jnp.moveaxis(blocks, 0, dim).reshape(lengths)
+
+
+def ring_gather(shard, axis, dim):
+    peers = lax.axis_size(axis)
+    pairs = [(i, (i + 1) % peers) for i in range(peers)]
+    back = [(b, a) for a, b in pairs]
+    lower, upper = ([], [])
+    for hop in range(peers - 1):
+        if hop % 2 == 0:
+            lower.append(lax.ppermute(lower[-1] if lower else shard, axis, pairs))
+        else:
+            upper.append(lax.ppermute(upper[-1] if upper else shard, axis, back))
+    blocks = jnp.stack([*lower[::-1], shard, *upper])
+    shift = lax.axis_index(axis) - len(lower)
+    blocks = blocks[(jnp.arange(peers) - shift) % peers]
+    return in_order(blocks, dim)
+
+
 def local(layer_input, queries, key_states, value_states, out_grad):
     local_rows = layer_input.shape[0]
     cycle_size = lax.axis_size("seq")
@@ -22,7 +44,7 @@
     scale = 1.0 / math.sqrt(HD)
     block = math.gcd(length, 512)
     key_all, value_all = (
-        lax.all_gather(key_states, "seq", axis=0, tiled=True),
+        ring_gather(key_states, "seq", 0),
         lax.all_gather(value_states, "seq", axis=0, tiled=True),
     )
     query_heads = queries.reshape(local_rows, KVH, group, HD)

time: 390 us -> 364 us (0.933)
  waiting for transfers between devices: 282 us -> 227 us
  starting transfers between devices: 31.2 us -> 48.5 us
  local copies, waits for them, and re-layouts: 34.5 us -> 46.9 us
    all_gather x1 -> x0, waiting for transfers between devices: 37 us -> none  [local(): lax.all_gather(key_states, 'seq', axis=0, tiled=True)]
    all_gather x1, waiting for transfers between devices: 41.1 us -> 11.8 us  [local(): lax.all_gather(value_states, 'seq', axis=0, tiled=True)]
    ppermute x0 -> x7, starting transfers between devices: none -> 17.3 us  [the longest x3 14.2 us: ring_gather(): upper.append(lax.ppermute(upper[-1] if upper else shard, axis, back))]
    ppermute x0 -> x7, waiting for transfers between devices: none -> 11.1 us  [the longest x4 11.1 us: ring_gather(): lower.append(lax.ppermute(lower[-1] if lower else shard, axis, pairs))]
    unnamed x12 -> x22, local copies, waits for them, and re-layouts: 15.9 us -> 22.5 us
  transfers between devices with their start and end apart: 6 -> 12, of which waited for: 5 -> 7; matrix products, arithmetic and copies ran while one was open for 5% -> 9% of each run, Pallas kernels for 0% -> 0%
where the time goes in v1:
time: 364 us
  waiting for transfers between devices  227 us (62%)
  starting transfers between devices  48.5 us (13%)
  local copies, waits for them, and re-layouts  46.9 us (13%)
  matrix products  21.8 us (6%)
  between operations  13.9 us (4%)
  other arithmetic  5.58 us (2%)
    reduce_scatter x1, waiting for transfers between devices, local(): lax.psum_scatter(terms, 'seq', scatter_dimension=0, tiled=True)  117 us
    all_gather x1, waiting for transfers between devices, local(): summed_grads = lax.all_gather(owned_grads, 'seq', axis=0, tiled=True)  47.2 us
    reduce_scatter x1, waiting for transfers between devices, local(): lax.psum_scatter(jnp.einsum('tr,tc->rc', columns, summed_grads, preferred...  39.4 us
    all_to_all x1, starting transfers between devices, local(): lax.all_to_all(layer_input.reshape(local_rows, replicas, cycle_size, slab...  30.8 us
    unnamed x22, local copies, waits for them, and re-layouts  22.5 us
    ppermute x3, starting transfers between devices, ring_gather(): upper.append(lax.ppermute(upper[-1] if upper else shard, axis, back))  14.2 us
    all_gather x1, waiting for transfers between devices, local(): lax.all_gather(value_states, 'seq', axis=0, tiled=True)  11.8 us
    ppermute x4, waiting for transfers between devices, ring_gather(): lower.append(lax.ppermute(lower[-1] if lower else shard, axis, pairs))  11.1 us
  transfers between devices with their start and end apart: 12, of which 7 were waited for; matrix products, arithmetic and copies ran while one was open for 9% of the time, Pallas kernels for 0%

profile of v1, /device:TPU:0, one launch (start us, length us, event | category | flops | bytes accessed | tf_op | source)
XLA Modules:
  0.0 363.5 jit_solution(8708284127801936568)
XLA Ops:
  7.2 3.0 collective-permute-start
  10.2 6.7 %collective-permute-done = bf16[128,512]{1,0:T(8,128)(2,1)S(1)} collective-permute-done((bf16[128,512]{1,0:T(8,128)(2,1)}, bf16[128,512]{1,0:T(8,128)(2,1)S(1)}, u32[]{:S(2)}, u32[]{:S(2)}) %collective-permute-start) | collective-permute-done | bytes 131104 | tf_op jit(solution)/shard_map/ppermute | solution.py:27
  17.0 4.7 %collective-permute-start.4 = (bf16[128,512]{1,0:T(8,128)(2,1)}, bf16[128,512]{1,0:T(8,128)(2,1)S(1)}, u32[]{:S(2)}, u32[]{:S(2)}) collective-permute-start(bf16[128,512]{1,0:T(8,128)(2,1)} %param.11), channel_id=1, source_target_pairs={{1,0},{2,1},{3,2},{4,3},{5,4},{6,5},{7,6},{0,7},{9,8},{10,9},{11,1... | collective-permute-start | bytes 393224 | tf_op jit(solution)/shard_map/ppermute | solution.py:29
  21.7 3.0 collective-permute-done.1
  24.7 1.7 copy.71
  26.5 4.7 %collective-permute-start.5 = (bf16[128,512]{1,0:T(8,128)(2,1)S(1)}, bf16[128,512]{1,0:T(8,128)(2,1)}, u32[]{:S(2)}, u32[]{:S(2)}) collective-permute-start(bf16[128,512]{1,0:T(8,128)(2,1)S(1)} %collective-permute-done.4), channel_id=1, source_target_pairs={{1,0},{2,1},{3,2},{4,3},{5,4},{6,5},{7,6},{0,7},{9,8},{10,9},{11,1... | collective-permute-start | bytes 393224 | tf_op jit(solution)/shard_map/ppermute | solution.py:29
  31.2 1.3 collective-permute-done.2
  32.6 1.6 copy.70
  34.9 1.6 copy.72
  36.5 1.3 copy.74
  37.9 4.8 %collective-permute-start.6 = (bf16[128,512]{1,0:T(8,128)(2,1)}, bf16[128,512]{1,0:T(8,128)(2,1)S(1)}, u32[]{:S(2)}, u32[]{:S(2)}) collective-permute-start(bf16[128,512]{1,0:T(8,128)(2,1)} %collective-permute-done.5), channel_id=1, source_target_pairs={{1,0},{2,1},{3,2},{4,3},{5,4},{6,5},{7,6},{0,7},{9,8},{10,9},{11,1... | collective-permute-start | bytes 393224 | tf_op jit(solution)/shard_map/ppermute | solution.py:29
  42.6 1.6 bitcast_dynamic-update-slice_fusion.7
  44.2 1.6 bitcast_dynamic-update-slice_fusion.6
  45.8 1.6 bitcast_dynamic-update-slice_fusion.5
  49.3 1.6 bitcast_dynamic-update-slice_fusion.1
  51.6 2.8 gather_fusion
  54.4 2.3 copy.93
  56.6 11.8 %all-gather.3.cloned.1.call-done = bf16[1024,512]{0,1:T(8,128)(2,1)} async-done(((bf16[128,512]{0,1:T(8,128)(2,1)}), bf16[1024,512]{0,1:T(8,128)(2,1)}) %all-gather.3.cloned.1.call-update) | async-done | bytes 1048592 | tf_op jit(solution)/shard_map/all_gather | solution.py:48
  68.4 7.5 %while.28 = (s32[]{:T(128)}, f32[4,8,128]{2,1,0:T(8,128)S(1)}, f32[4,8,128]{2,1,0:T(8,128)S(1)}, f32[4,8,128]{2,1,0:T(8,128)S(1)}, s32[]{:T(128)}, /*index=5*/bf...) while((s32[]{:T(128)}, f32[4,8,128]{2,1,0:T(8,128)S(1)}, ...), condition=%wide.region_4.5_spmd.clone, body=%wide.region_0.4_spmd.clone.sunk | while | flops 1098986112 | bytes 35165400 | solution.py:88
  68.4 1.3 constant_dynamic-slice_fusion.6
  69.9 1.5 fusion.59
  71.4 1.8 fusion.61
  73.2 2.7 fusion.60
  76.0 2.5 broadcast_in_dim.33.clone
  78.4 1.6 broadcast_in_dim.32
  80.1 19.8 %while.29 = (s32[]{:T(128)}, f32[128,4,8,128]{0,3,2,1:T(8,128)}, f32[1024,1024]{1,0:T(8,128)}, s32[]{:T(128)}, bf16[1024,512]{0,1:T(8,128)(2,1)}, /*index=5*/bf1...) while((s32[]{:T(128)}, f32[128,4,8,128]{0,3,2,1:T(8,128)}, ...), condition=%wide.region_6.7_spmd.clone, body=%wide.region_5.6_spmd.clone.sunk | while | flops 2704343552 | bytes 108713312 | solution.py:117
  80.1 1.6 constant_dynamic-slice_fusion.7
  81.9 2.3 fusion.72
  84.2 1.7 fusion.73
  85.9 1.5 fusion.75
  87.9 1.5 fusion.74
  89.4 1.5 pad_maximum_fusion.2
  90.9 1.9 copy.111
  92.8 1.5 constant_dynamic-update-slice_fusion.2
  94.3 1.5 copy-done.1
  95.8 4.1 %bitcast_add_fusion.2 = f32[128,4,8,128]{0,3,2,1:T(8,128)} fusion(f32[128,4,8,128]{0,3,2,1:T(8,128)} %get-tuple-element.501, bf16[512,4,128,1]{0,2,3,1:T(8,128)(2,1)} %bitcast.172, bf16[4,8,128,512]{2,3,1,0:T(8,128)(2,1)S(1)} %copy-done.1), kind=kOutput, calls=%fused_computation.27.clone.1 | convolution fusion | flops 537395200 | bytes 8912896 | tf_op jit(solution)/shard_map/while/body/kgts,skd->tkgd/dot_general | solution.py:98
  99.9 3.2 copy.77
  103.2 1.5 copy.78
  104.7 30.8 %all-to-all-start = ((bf16[128,4,8,256]{0,3,1,2:T(8,128)(2,1)}), bf16[128,4,8,256]{0,3,1,2:T(8,128)(2,1)S(1)}, u32[]{:S(2)}, u32[]{:S(2)}) async-start(bf16[128,4,8,256]{0,3,1,2:T(8,128)(2,1)} %copy.78), calls=%async_computation.1 | async-start | bytes 4194304 | tf_op jit(solution)/shard_map/all_to_all | solution.py:124
  135.6 117.1 %reduce-scatter.3.cloned.1.call-done = f32[128,1024]{1,0:T(8,128)} async-done(((f32[1024,1024]{1,0:T(8,128)}), f32[128,1024]{1,0:T(8,128)}) %reduce-scatter.3.cloned.1.call-update) | async-done | bytes 524304 | tf_op jit(solution)/shard_map/reduce_scatter | solution.py:119
  252.7 1.8 convert_element_type.17
  254.8 2.7 copy.79
  257.5 47.2 %all-gather.5.cloned.1.call-done = bf16[1024,1024]{1,0:T(8,128)(2,1)} async-done(((bf16[128,1024]{1,0:T(8,128)(2,1)}), bf16[1024,1024]{1,0:T(8,128)(2,1)}) %all-gather.5.cloned.1.call-update) | async-done | bytes 2097168 | tf_op jit(solution)/shard_map/all_gather | solution.py:122
  304.7 6.5 %convolution_bitcast_fusion = f32[1024,1024]{0,1:T(8,128)} fusion(bf16[1024,1024]{1,0:T(8,128)(2,1)} %all-gather.5.cloned.1.call-done, bf16[128,8,8,128]{3,2,1,0:T(8,128)(2,1)} %bitcast.179), kind=kOutput, calls=%fused_computation.34 | convolution fusion | flops 2147483648 | bytes 8388608 | tf_op jit(solution)/shard_map/tr,tc->rc/dot_general | solution.py:133
  311.3 1.6 copy-done.2
  313.0 1.3 copy.94
  315.0 39.4 %reduce-scatter.5.cloned.1.call-done = f32[256,1024]{0,1:T(8,128)} async-done(((f32[1024,1024]{0,1:T(8,128)}), f32[256,1024]{0,1:T(8,128)}) %reduce-scatter.5.cloned.1.call-update) | async-done | bytes 1048592 | tf_op jit(solution)/shard_map/reduce_scatter | solution.py:132
  354.4 2.5 copy.80
  (56 shorter events, 5.6 us)
Async XLA Ops:
  7.2 61.3 %all-gather.3.cloned.1.call-start = ((), (), s32[]{:S(2)}) async-start(), calls=%async_computation.3 | async-start | bytes 1179648 | tf_op jit(solution)/shard_map/all_gather | solution.py:48
  7.2 9.7 %collective-permute-start = (bf16[128,512]{1,0:T(8,128)(2,1)}, bf16[128,512]{1,0:T(8,128)(2,1)S(1)}, u32[]{:S(2)}, u32[]{:S(2)}) collective-permute-start(bf16[128,512]{1,0:T(8,128)(2,1)} %param.11), channel_id=1, source_target_pairs={{0,1},{1,2},{2,3},{3,4},{4,5},{5,6},{6,7},{7,0},{8,9},{9,10},{10,1... | collective-permute-start | bytes 393224 | tf_op jit(solution)/shard_map/ppermute | solution.py:27
  16.9 7.7 %collective-permute-start.1 = (bf16[128,512]{1,0:T(8,128)(2,1)S(1)}, bf16[128,512]{1,0:T(8,128)(2,1)S(1)}, u32[]{:S(2)}, u32[]{:S(2)}) collective-permute-start(bf16[128,512]{1,0:T(8,128)(2,1)S(1)} %collective-permute-done), channel_id=1, source_target_pairs={{0,1},{1,2},{2,3},{3,4},{4,5},{5,6},{6,7},{7,0},{8,9},{9,10},{10,1... | collective-permute-start | bytes 393224 | tf_op jit(solution)/shard_map/ppermute | solution.py:27
  17.0 9.5 %collective-permute-start.4 = (bf16[128,512]{1,0:T(8,128)(2,1)}, bf16[128,512]{1,0:T(8,128)(2,1)S(1)}, u32[]{:S(2)}, u32[]{:S(2)}) collective-permute-start(bf16[128,512]{1,0:T(8,128)(2,1)} %param.11), channel_id=1, source_target_pairs={{1,0},{2,1},{3,2},{4,3},{5,4},{6,5},{7,6},{0,7},{9,8},{10,9},{11,1... | collective-permute-start | bytes 393224 | tf_op jit(solution)/shard_map/ppermute | solution.py:29
  24.7 9.5 %copy-start.9 = (bf16[128,512]{1,0:T(8,128)(2,1)}, bf16[128,512]{1,0:T(8,128)(2,1)S(1)}, u32[]{:S(2)}) copy-start(bf16[128,512]{1,0:T(8,128)(2,1)S(1)} %collective-permute-done.1) | copy-start | bytes 393220
  24.7 7.9 %collective-permute-start.2 = (bf16[128,512]{1,0:T(8,128)(2,1)S(1)}, bf16[128,512]{1,0:T(8,128)(2,1)}, u32[]{:S(2)}, u32[]{:S(2)}) collective-permute-start(bf16[128,512]{1,0:T(8,128)(2,1)S(1)} %collective-permute-done.1), channel_id=1, source_target_pairs={{0,1},{1,2},{2,3},{3,4},{4,5},{5,6},{6,7},{7,0},{8,9},{9,10},{10,1... | collective-permute-start | bytes 393224 | tf_op jit(solution)/shard_map/ppermute | solution.py:27
  26.4 226.3 %reduce-scatter.3.cloned.1.call-start = ((), (), s32[]{:S(2)}) async-start(), calls=%async_computation.4 | async-start | bytes 4718592 | tf_op jit(solution)/shard_map/reduce_scatter | solution.py:119
  26.5 11.4 %collective-permute-start.5 = (bf16[128,512]{1,0:T(8,128)(2,1)S(1)}, bf16[128,512]{1,0:T(8,128)(2,1)}, u32[]{:S(2)}, u32[]{:S(2)}) collective-permute-start(bf16[128,512]{1,0:T(8,128)(2,1)S(1)} %collective-permute-done.4), channel_id=1, source_target_pairs={{1,0},{2,1},{3,2},{4,3},{5,4},{6,5},{7,6},{0,7},{9,8},{10,9},{11,1... | collective-permute-start | bytes 393224 | tf_op jit(solution)/shard_map/ppermute | solution.py:29
  32.5 10.1 %collective-permute-start.3 = (bf16[128,512]{1,0:T(8,128)(2,1)}, bf16[128,512]{1,0:T(8,128)(2,1)}, u32[]{:S(2)}, u32[]{:S(2)}) collective-permute-start(bf16[128,512]{1,0:T(8,128)(2,1)} %collective-permute-done.2), channel_id=1, source_target_pairs={{0,1},{1,2},{2,3},{3,4},{4,5},{5,6},{6,7},{7,0},{8,9},{9,10},{10,1... | collective-permute-start | bytes 393224 | tf_op jit(solution)/shard_map/ppermute | solution.py:27
  34.2 13.8 %copy-start.8 = (bf16[128,512]{1,0:T(8,128)(2,1)S(1)}, bf16[128,512]{1,0:T(8,128)(2,1)}, u32[]{:S(2)}) copy-start(bf16[128,512]{1,0:T(8,128)(2,1)} %param.11) | copy-start | bytes 393220
  37.9 13.0 %collective-permute-start.6 = (bf16[128,512]{1,0:T(8,128)(2,1)}, bf16[128,512]{1,0:T(8,128)(2,1)S(1)}, u32[]{:S(2)}, u32[]{:S(2)}) collective-permute-start(bf16[128,512]{1,0:T(8,128)(2,1)} %collective-permute-done.5), channel_id=1, source_target_pairs={{1,0},{2,1},{3,2},{4,3},{5,4},{6,5},{7,6},{0,7},{9,8},{10,9},{11,1... | collective-permute-start | bytes 393224 | tf_op jit(solution)/shard_map/ppermute | solution.py:29
  71.4 1.8 copy-start.7
  80.1 5.8 %copy-start.3 = (bf16[128,4,8,128]{0,3,2,1:T(8,128)(2,1)}, bf16[128,4,8,128]{0,3,2,1:T(8,128)(2,1)S(1)}, u32[]{:S(2)}) copy-start(bf16[128,4,8,128]{0,3,2,1:T(8,128)(2,1)S(1)} %get-tuple-element.521) | copy-start | bytes 3145732 | tf_op jit(solution)/shard_map/while
  81.7 2.5 copy-start.5
  85.9 2.0 copy-start
  92.8 2.9 copy-start.1
  95.8 4.1 %copy-start.4 = (bf16[128,4,8,128]{0,3,2,1:T(8,128)(2,1)S(1)}, bf16[128,4,8,128]{0,3,2,1:T(8,128)(2,1)}, u32[]{:S(2)}) copy-start(bf16[128,4,8,128]{0,3,2,1:T(8,128)(2,1)} %copy-done.3) | copy-start | bytes 3145732 | tf_op jit(solution)/shard_map/while
  104.7 150.1 %all-to-all-start = ((bf16[128,4,8,256]{0,3,1,2:T(8,128)(2,1)}), bf16[128,4,8,256]{0,3,1,2:T(8,128)(2,1)S(1)}, u32[]{:S(2)}, u32[]{:S(2)}) async-start(bf16[128,4,8,256]{0,3,1,2:T(8,128)(2,1)} %copy.78), calls=%async_computation.1 | async-start | bytes 4194304 | tf_op jit(solution)/shard_map/all_to_all | solution.py:124
  135.5 169.2 %all-gather.5.cloned.1.call-start = ((), (), s32[]{:S(2)}) async-start(), calls=%async_computation.5 | async-start | bytes 2359296 | tf_op jit(solution)/shard_map/all_gather | solution.py:122
  254.5 99.9 %reduce-scatter.5.cloned.1.call-start = ((), (), s32[]{:S(2)}) async-start(), calls=%async_computation.6 | async-start | bytes 5242880 | tf_op jit(solution)/shard_map/reduce_scatter | solution.py:132
  311.3 1.6 copy-start.2
  311.3 3.1 copy-start.6
Sparse Core Ops, SparseCore 0:
  26.5 41.8 all-gather.2
  100.0 152.6 reduce-scatter.2
  255.6 49.0 all-gather.4
  311.4 42.9 reduce-scatter.4
